TPU v7x, 512 devices: a whole 4x8x8 slice. The times are simulated.
512 devices in a mesh: rep: 32 (over z, x), tp: 16 (over y, core).
Axes of the slice: x: 4, y: 8, z: 8, core: 2. Of those that a mesh axis runs over, the one named last changes fastest.
Arguments:
- tokens: bfloat16 [16384, 8192], P('rep', 'tp'), may hold values from -6 to 6
- frozen_weight: bfloat16 [8192, 2048], P('tp'), may hold values from -0.0625 to 0.0625
- cotangent: bfloat16 [16384, 2048], P('rep', 'tp'), may hold values from -6 to 6
- adapter_input_maps: bfloat16 [32, 16, 8192], P('rep', None, 'tp'), may hold values from -0.0625 to 0.0625
- adapter_output_maps: bfloat16 [32, 16, 2048], P('rep', None, 'tp'), may hold values from -0.375 to 0.375
- tenant: int32 [128], P('rep'), may hold values from 0 to 31
- adapter_storage_slot: int32 [32], replicated, may hold values from 0 to 31, each once
Outputs:
- projected: float32 [16384, 2048], P('rep', 'tp')
- token_gradient: float32 [16384, 8192], P('rep', 'tp')
- adapter_input_gradient: float32 [32, 16, 8192], P('rep', None, 'tp')
- adapter_output_gradient: float32 [32, 16, 2048], P('rep', None, 'tp')
Inputs may be any that keep to these rules, and one draw needn't show every extreme that they name: `adapter_storage_slot`: each slot holds exactly one adapter.
All inputs are finite; a program needn't handle non-finite values.
Results may differ from a plain program's by a relative error of at most 0.00035.
Values may be sent and summed in bfloat16 or wider, within the bound.
A program may use at most 64 MiB of HBM per device.

v0:
```python
import jax
import jax.numpy as jnp
from jax import lax
from jax.sharding import PartitionSpec as P

HIGH_ACCURACY = lax.Precision.HIGHEST


def slot_lookup(tenants, adapter_storage_slot):
    labels = jnp.arange(adapter_storage_slot.shape[0], dtype=jnp.int32)
    return jnp.sum(
        jnp.where(tenants[:, None] == labels[None, :], adapter_storage_slot[None, :], 0), axis=1
    )


def shards(
    tokens,
    frozen_weight,
    cotangent,
    adapter_input_maps,
    adapter_output_maps,
    tenant,
    adapter_storage_slot,
):
    token_count = tokens.shape[0]
    blocks = tenant.shape[0]
    block_len = token_count // blocks
    tenant_token_count = adapter_input_maps.shape[0]
    inputs_all, outputs_all = (
        lax.all_gather(adapter_input_maps, "rep", axis=0, tiled=True),
        lax.all_gather(adapter_output_maps, "rep", axis=0, tiled=True),
    )
    adapter_list = inputs_all.shape[0]
    labels = jnp.arange(adapter_list, dtype=jnp.int32)
    block_storage_slot = slot_lookup(tenant, adapter_storage_slot)
    tenant_selector = (block_storage_slot[:, None] == labels[None, :]).astype(jnp.float32)
    picker = tenant_selector.astype(jnp.bfloat16)
    input_map_rows = jnp.einsum(
        "bs,srd->brd", picker, inputs_all, preferred_element_type=jnp.float32
    )
    output_map_rows = jnp.einsum(
        "bs,src->brc", picker, outputs_all, preferred_element_type=jnp.float32
    )
    token_rows = tokens.reshape(blocks, block_len, -1).astype(jnp.float32)
    grad_rows = cotangent.reshape(blocks, block_len, -1).astype(jnp.float32)
    part_in = jnp.einsum("bnd,brd->bnr", token_rows, input_map_rows, precision=HIGH_ACCURACY)
    part_back = jnp.einsum("bnc,brc->bnr", grad_rows, output_map_rows, precision=HIGH_ACCURACY)
    rank_in, rank_back = lax.psum((part_in, part_back), "tp")
    base_terms = jnp.dot(tokens, frozen_weight, preferred_element_type=jnp.float32)
    base = lax.psum_scatter(base_terms, "tp", scatter_dimension=1, tiled=True)
    low_rank = 2.0 * jnp.einsum("bnr,brc->bnc", rank_in, output_map_rows, precision=HIGH_ACCURACY)
    projected = base + low_rank.reshape(token_count, -1)
    through = lax.dot_general(
        lax.all_gather(cotangent, "tp", axis=1, tiled=True),
        frozen_weight,
        (((1,), (1,)), ((), ())),
        preferred_element_type=jnp.float32,
    )
    side = 2.0 * jnp.einsum("bnr,brd->bnd", rank_back, input_map_rows, precision=HIGH_ACCURACY)
    token_gradient = through + side.reshape(token_count, -1)
    input_map_gradient = 2.0 * jnp.einsum(
        "bnr,bnd->brd", rank_back, token_rows, precision=HIGH_ACCURACY
    )
    output_map_gradient = 2.0 * jnp.einsum(
        "bnr,bnc->brc", rank_in, grad_rows, precision=HIGH_ACCURACY
    )
    every_tenant = lax.all_gather(tenant, "rep", axis=0, tiled=True)
    every_slot = slot_lookup(every_tenant, adapter_storage_slot)
    owned = lax.axis_index("rep") * tenant_token_count + jnp.arange(
        tenant_token_count, dtype=jnp.int32
    )
    owner_select = (every_slot[:, None] == owned[None, :]).astype(jnp.float32)
    counts = block_len * jnp.sum(owner_select, axis=0)
    adapter_scale = 1.0 / jnp.maximum(counts, 1.0)
    table_in = jnp.einsum(
        "ol,oht->lht", tenant_selector, input_map_gradient, precision=HIGH_ACCURACY
    )
    table_out = jnp.einsum(
        "pa,pne->ane", tenant_selector, output_map_gradient, precision=HIGH_ACCURACY
    )
    input_gradient_sum, output_gradient_sum = (
        lax.psum_scatter(table_in, "rep", scatter_dimension=0, tiled=True),
        lax.psum_scatter(table_out, "rep", scatter_dimension=0, tiled=True),
    )
    adapter_input_gradient = input_gradient_sum * adapter_scale[:, None, None]
    adapter_output_gradient = output_gradient_sum * adapter_scale[:, None, None]
    return (projected, token_gradient, adapter_input_gradient, adapter_output_gradient)


def solution(mesh):
    placed = (
        P("rep", "tp"),
        P("tp", None),
        P("rep", "tp"),
        P("rep", None, "tp"),
        P("rep", None, "tp"),
        P("rep"),
        P(),
    )
    return jax.shard_map(
        shards,
        mesh=mesh,
        in_specs=placed,
        out_specs=(P("rep", "tp"), P("rep", "tp"), P("rep", None, "tp"), P("rep", None, "tp")),
        check_vma=False,
    )
```

profile of v0, /device:TPU:25, one launch (start us, length us, event | category | flops | bytes accessed | tf_op | source)
XLA Modules:
  0.0 783.0 jit_solution(3900021885987403363)
XLA Ops:
  7.2 0.0 copy-start
  7.2 0.0 copy-start.1
  7.2 0.0 copy-start.2
  7.2 0.0 all-reduce.4.cloned.1.call-start
  7.2 43.7 %all_gather.12 = bf16[32,16,512]{2,1,0:T(8,128)(2,1)S(1)} all-gather(bf16[1,16,512]{2,1,0:T(8,128)(2,1)} %param.10), channel_id=1, replica_groups=mesh['rep'=32,'tp'=16] {'rep'}, dimensions={0}, use_global_device_ids=true | all-gather | bytes 540672 | tf_op jit(solution)/shard_map/all_gather | solution.py:30
  50.9 32.8 %all_gather.13 = bf16[32,16,128]{2,1,0:T(8,128)(2,1)S(1)} all-gather(bf16[1,16,128]{2,1,0:T(8,128)(2,1)} %param.11), channel_id=1, replica_groups=mesh['rep'=32,'tp'=16] {'rep'}, dimensions={0}, use_global_device_ids=true | all-gather | bytes 135168 | tf_op jit(solution)/shard_map/all_gather | solution.py:31
  83.8 0.9 select_reduce_fusion.1
  84.6 0.4 fusion
  85.0 0.2 fusion.4
  85.2 2.2 convolution_bitcast_fusion.1
  87.4 0.0 copy-done.2
  87.4 0.9 convolution_bitcast_fusion
  88.3 0.0 all-reduce.4.cloned.1.call-update
  88.4 0.0 reduce-scatter.8.cloned.1.call-start
  88.4 124.0 %all-reduce.4.cloned.1.call-done = (f32[4,128,16]{1,2,0:T(8,128)}, f32[4,128,16]{1,2,0:T(8,128)}) async-done(((f32[4,128,16]{1,2,0:T(8,128)}, f32[4,128,16]{1,2,0:T(8,128)}), (f32[4,128,16]{1,2,0:T(8,128)}, f32[4,128,16]{1,2,0:T(8,128)})) %all-reduce.4.cloned.1.call-update) | async-done | bytes 65552 | tf_op jit(solution)/shard_map/psum | solution.py:48
  212.4 1.0 convolution_multiply_fusion.3
  213.4 0.4 fusion.8
  213.8 0.9 copy.36
  214.7 0.0 reduce-scatter.8.cloned.1.call-update
  214.7 0.0 reduce-scatter.6.cloned.1.call-start
  214.8 0.0 copy-done.1
  214.8 1.1 convolution_multiply_fusion.2
  215.8 0.7 fusion.2
  216.6 1.6 copy.34
  218.2 0.0 reduce-scatter.6.cloned.1.call-update
  218.2 0.0 all-gather.2.cloned.1.call-start
  218.2 0.5 all-gather.2.cloned.1.call-update
  218.8 0.0 reduce-scatter.4.cloned.1.call-start
  218.8 0.0 copy-done
  218.8 3.2 fusion.23
  222.0 0.0 copy-start.5
  222.0 0.0 copy-start.6
  222.0 0.0 copy-start.3
  222.0 0.0 copy-start.4
  222.0 0.0 reduce-scatter.4.cloned.1.call-update
  222.1 1.3 dynamic-slice
  224.0 0.0 copy-done.5
  224.0 0.2 dynamic-update-slice
  224.3 17.4 %all-reduce = s32[128]{0:T(128)S(1)} all-reduce(s32[128]{0:T(128)S(1)} %dynamic-update-slice), channel_id=1, replica_groups=mesh['rep'=32,'tp'=16] {'rep'}, use_global_device_ids=true, to_apply=%add | all-reduce | flops 128 | bytes 1024
  241.6 0.0 copy-done.6
  241.6 0.1 select_reduce_fusion
  241.7 0.6 fusion.22
  243.0 0.0 copy-done.3
  243.0 0.6 convolution_multiply_fusion.1
  243.6 0.0 copy-done.4
  243.6 2.0 convolution_multiply_fusion
  245.7 187.2 %reduce-scatter.8.cloned.1.call-done = f32[1,16,128]{2,1,0:T(8,128)} async-done(((f32[32,16,128]{2,1,0:T(8,128)}), f32[1,16,128]{2,1,0:T(8,128)}) %reduce-scatter.8.cloned.1.call-update) | async-done | bytes 8208 | tf_op jit(solution)/shard_map/reduce_scatter | solution.py:83
  432.9 1.3 broadcast_multiply_fusion.1
  434.2 224.1 %reduce-scatter.6.cloned.1.call-done = f32[1,16,512]{2,1,0:T(8,128)} async-done(((f32[32,16,512]{2,1,0:T(8,128)}), f32[1,16,512]{2,1,0:T(8,128)}) %reduce-scatter.6.cloned.1.call-update) | async-done | bytes 32784 | tf_op jit(solution)/shard_map/reduce_scatter | solution.py:82
  658.3 1.4 broadcast_multiply_fusion
  659.7 46.8 %all-gather.2.cloned.1.call-done = bf16[512,2048]{1,0:T(8,128)(2,1)} async-done(((bf16[512,128]{1,0:T(8,128)(2,1)}), bf16[512,2048]{1,0:T(8,128)(2,1)}) %all-gather.2.cloned.1.call-update) | async-done | bytes 2097168 | tf_op jit(solution)/shard_map/all_gather | solution.py:54
  706.5 4.1 convolution_add_fusion
  710.6 64.2 %reduce-scatter.4.cloned.1.call-done = f32[512,128]{1,0:T(8,128)} async-done(((f32[512,2048]{1,0:T(8,128)}), f32[512,128]{1,0:T(8,128)}) %reduce-scatter.4.cloned.1.call-update) | async-done | bytes 262160 | tf_op jit(solution)/shard_map/reduce_scatter | solution.py:50
  774.8 1.7 bitcast_add_fusion
  (1 shorter events, 0.0 us)
Async XLA Ops:
  7.2 211.7 %copy-start = (bf16[512,2048]{1,0:T(8,128)(2,1)S(1)}, bf16[512,2048]{1,0:T(8,128)(2,1)}, u32[]{:S(2)}) copy-start(bf16[512,2048]{1,0:T(8,128)(2,1)} %param.8) | copy-start | bytes 6291460
  7.2 207.6 %copy-start.1 = (bf16[512,512]{1,0:T(8,128)(2,1)S(1)}, bf16[512,512]{1,0:T(8,128)(2,1)}, u32[]{:S(2)}) copy-start(bf16[512,512]{1,0:T(8,128)(2,1)} %param.7) | copy-start | bytes 1572868
  7.2 80.2 %copy-start.2 = (bf16[512,128]{1,0:T(8,128)(2,1)S(1)}, bf16[512,128]{1,0:T(8,128)(2,1)}, u32[]{:S(2)}) copy-start(bf16[512,128]{1,0:T(8,128)(2,1)} %param.9) | copy-start | bytes 393220
  7.2 205.2 %all-reduce.4.cloned.1.call-start = ((), (), s32[]{:S(2)}) async-start(), calls=%async_computation.7 | async-start | bytes 131072 | tf_op jit(solution)/shard_map/psum | solution.py:48
  88.4 344.5 %reduce-scatter.8.cloned.1.call-start = ((), (), s32[]{:S(2)}) async-start(), calls=%async_computation.6 | async-start | bytes 270336 | tf_op jit(solution)/shard_map/reduce_scatter | solution.py:83
  214.7 443.6 %reduce-scatter.6.cloned.1.call-start = ((), (), s32[]{:S(2)}) async-start(), calls=%async_computation.5 | async-start | bytes 1081344 | tf_op jit(solution)/shard_map/reduce_scatter | solution.py:82
  218.2 488.3 %all-gather.2.cloned.1.call-start = ((), (), s32[]{:S(2)}) async-start(), calls=%async_computation.4 | async-start | bytes 2228224 | tf_op jit(solution)/shard_map/all_gather | solution.py:54
  218.8 556.1 %reduce-scatter.4.cloned.1.call-start = ((), (), s32[]{:S(2)}) async-start(), calls=%async_computation.3 | async-start | bytes 4456448 | tf_op jit(solution)/shard_map/reduce_scatter | solution.py:50
  222.0 2.0 copy-start.5
  222.0 19.6 %copy-start.6 = (s32[32]{0:T(128)S(1)}, s32[32]{0:T(128)}, u32[]{:S(2)}) copy-start(s32[32]{0:T(128)} %param.13) | copy-start | bytes 388
  222.0 21.0 %copy-start.3 = (f32[4,128,16]{1,2,0:T(8,128)S(1)}, f32[4,128,16]{1,2,0:T(8,128)}, u32[]{:S(2)}) copy-start(f32[4,128,16]{1,2,0:T(8,128)} %get-tuple-element.8) | copy-start | bytes 98308
  222.0 21.6 %copy-start.4 = (f32[4,128,16]{1,2,0:T(8,128)S(1)}, f32[4,128,16]{1,2,0:T(8,128)}, u32[]{:S(2)}) copy-start(f32[4,128,16]{1,2,0:T(8,128)} %get-tuple-element.9) | copy-start | bytes 98308
Sparse Core Ops, SparseCore 0:
  88.5 123.9 all-reduce.3
  217.4 215.4 reduce-scatter.7
  437.3 220.9 reduce-scatter.5
  660.2 46.2 all-gather.1
  709.2 65.6 reduce-scatter.3
where the time goes:
time: 784 us; the launch traced here: 783 us
  waiting for transfers between devices  647 us (83%)
  blocking collectives  93.9 us (12%)
  matrix products  16.8 us (2%)
  between operations  15.2 us (2%)
    reduce_scatter x1, waiting for transfers between devices, shards(): lax.psum_scatter(table_in, 'rep', scatter_dimension=0, tiled=True)  224 us
    reduce_scatter x1, waiting for transfers between devices, shards(): lax.psum_scatter(table_out, 'rep', scatter_dimension=0, tiled=True)  187 us
    psum x1, waiting for transfers between devices, shards(): rank_in, rank_back = lax.psum((part_in, part_back), 'tp')  124 us
    reduce_scatter x1, waiting for transfers between devices, shards(): base = lax.psum_scatter(base_terms, 'tp', scatter_dimension=1, tiled=True)  64.2 us
    all_gather x1, waiting for transfers between devices, shards(): lax.all_gather(cotangent, 'tp', axis=1, tiled=True)  46.8 us
    all_gather x1, blocking collectives, shards(): lax.all_gather(adapter_input_maps, 'rep', axis=0, tiled=True)  43.7 us
    all_gather x1, blocking collectives, shards(): lax.all_gather(adapter_output_maps, 'rep', axis=0, tiled=True)  32.8 us
    unnamed x1, blocking collectives  17.4 us
  transfers between devices with their start and end apart: 5, of which 5 were waited for; matrix products, arithmetic and copies ran while one was open for 2% of the time, Pallas kernels for 0%

commit v1 on v0

--- a/solution.py
+++ b/solution.py
@@ -2,8 +2,19 @@
 import jax.numpy as jnp
 from jax import lax
 from jax.sharding import PartitionSpec as P
+from jax.lax import all_to_all, axis_size
 
 HIGH_ACCURACY = lax.Precision.HIGHEST
+
+
+def update_strings(message, bus_axis):
+    current_value = all_to_all(
+        jnp.stack([message for _ in range(axis_size(bus_axis))], axis=0),
+        axis_name=bus_axis,
+        split_axis=0,
+        concat_axis=0,
+    )
+    return jnp.concatenate(current_value, axis=0)
 
 
 def slot_lookup(tenants, adapter_storage_slot):
@@ -28,7 +39,7 @@
     tenant_token_count = adapter_input_maps.shape[0]
     inputs_all, outputs_all = (
         lax.all_gather(adapter_input_maps, "rep", axis=0, tiled=True),
-        lax.all_gather(adapter_output_maps, "rep", axis=0, tiled=True),
+        update_strings(adapter_output_maps, "rep"),
     )
     adapter_list = inputs_all.shape[0]
     labels = jnp.arange(adapter_list, dtype=jnp.int32)

time: 784 us -> 753 us (0.960)
  blocking collectives: 93.9 us -> 56 us
  starting transfers between devices: 0.2 us -> 13.1 us
    all_gather x1 -> x0, blocking collectives: 32.8 us -> none  [shards(): lax.all_gather(adapter_output_maps, 'rep', axis=0, tiled=True)]
    all_to_all x0 -> x1, starting transfers between devices: none -> 12.9 us  [update_strings(): all_to_all(jnp.stack([message for _ in range(axis_size(bus_axis))], axis=...]
  transfers between devices with their start and end apart: 5 -> 6, of which waited for: 5 -> 5; matrix products, arithmetic and copies ran while one was open for 2% -> 3% of each run, Pallas kernels for 0% -> 0%
where the time goes in v1:
time: 753 us; the launch traced here: 752 us
  waiting for transfers between devices  640 us (85%)
  blocking collectives  56 us (7%)
  matrix products  16.8 us (2%)
  between operations  15.2 us (2%)
  starting transfers between devices  13.1 us (2%)
    reduce_scatter x1, waiting for transfers between devices, shards(): lax.psum_scatter(table_in, 'rep', scatter_dimension=0, tiled=True)  224 us
    reduce_scatter x1, waiting for transfers between devices, shards(): lax.psum_scatter(table_out, 'rep', scatter_dimension=0, tiled=True)  187 us
    psum x1, waiting for transfers between devices, shards(): rank_in, rank_back = lax.psum((part_in, part_back), 'tp')  117 us
    reduce_scatter x1, waiting for transfers between devices, shards(): base = lax.psum_scatter(base_terms, 'tp', scatter_dimension=1, tiled=True)  64.2 us
    all_gather x1, waiting for transfers between devices, shards(): lax.all_gather(cotangent, 'tp', axis=1, tiled=True)  46.8 us
    all_gather x1, blocking collectives, shards(): lax.all_gather(adapter_input_maps, 'rep', axis=0, tiled=True)  38.7 us
    unnamed x1, blocking collectives  17.4 us
  transfers between devices with their start and end apart: 6, of which 5 were waited for; matrix products, arithmetic and copies ran while one was open for 3% of the time, Pallas kernels for 0%

profile of v1, /device:TPU:25, one launch (start us, length us, event | category | flops | bytes accessed | tf_op | source)
XLA Modules:
  0.0 752.3 jit_solution(1125637772667302773)
XLA Ops:
  7.2 0.0 copy-start
  7.2 0.0 copy-start.1
  7.2 0.0 copy-start.2
  7.2 1.5 stack.2
  8.7 12.9 %all-to-all-start = ((bf16[32,1,16,128]{3,2,1,0:T(8,128)(2,1)}), bf16[32,1,16,128]{3,2,1,0:T(8,128)(2,1)S(1)}, u32[]{:S(2)}, u32[]{:S(2)}) async-start(bf16[32,1,16,128]{3,2,1,0:T(8,128)(2,1)} %stack.2), calls=%async_computation.1 | async-start | bytes 262144 | tf_op jit(solution)/shard_map/all_to_all | solution.py:11
  21.6 0.0 all-reduce.4.cloned.1.call-start
  21.7 38.7 %all_gather.9 = bf16[32,16,512]{2,1,0:T(8,128)(2,1)S(1)} all-gather(bf16[1,16,512]{2,1,0:T(8,128)(2,1)} %param.10), channel_id=1, replica_groups=mesh['rep'=32,'tp'=16] {'rep'}, dimensions={0}, use_global_device_ids=true | all-gather | bytes 540672 | tf_op jit(solution)/shard_map/all_gather | solution.py:41
  60.3 0.9 select_reduce_fusion.1
  61.2 0.4 fusion
  61.6 2.2 convolution_bitcast_fusion.1
  63.8 0.0 all-to-all-done
  63.8 0.2 fusion.2
  64.0 0.0 copy-done.2
  64.0 0.9 convolution_bitcast_fusion
  64.9 0.0 all-reduce.4.cloned.1.call-update
  64.9 0.0 reduce-scatter.8.cloned.1.call-start
  65.0 116.7 %all-reduce.4.cloned.1.call-done = (f32[4,128,16]{1,2,0:T(8,128)}, f32[4,128,16]{1,2,0:T(8,128)}) async-done(((f32[4,128,16]{1,2,0:T(8,128)}, f32[4,128,16]{1,2,0:T(8,128)}), (f32[4,128,16]{1,2,0:T(8,128)}, f32[4,128,16]{1,2,0:T(8,128)})) %all-reduce.4.cloned.1.call-update) | async-done | bytes 65552 | tf_op jit(solution)/shard_map/psum | solution.py:59
  181.7 1.0 convolution_multiply_fusion.3
  182.7 0.4 fusion.9
  183.1 0.9 copy.35
  184.0 0.0 reduce-scatter.8.cloned.1.call-update
  184.0 0.0 reduce-scatter.6.cloned.1.call-start
  184.1 0.0 copy-done.1
  184.1 1.1 convolution_multiply_fusion.2
  185.1 0.7 fusion.4
  185.9 1.6 copy.33
  187.5 0.0 reduce-scatter.6.cloned.1.call-update
  187.5 0.0 all-gather.2.cloned.1.call-start
  187.5 0.5 all-gather.2.cloned.1.call-update
  188.1 0.0 reduce-scatter.4.cloned.1.call-start
  188.1 0.0 copy-done
  188.1 3.2 fusion.24
  191.3 0.0 copy-start.5
  191.3 0.0 copy-start.6
  191.3 0.0 copy-start.3
  191.3 0.0 copy-start.4
  191.3 0.0 reduce-scatter.4.cloned.1.call-update
  191.4 1.3 dynamic-slice
  193.3 0.0 copy-done.5
  193.3 0.2 dynamic-update-slice
  193.6 17.4 %all-reduce = s32[128]{0:T(128)S(1)} all-reduce(s32[128]{0:T(128)S(1)} %dynamic-update-slice), channel_id=1, replica_groups=mesh['rep'=32,'tp'=16] {'rep'}, use_global_device_ids=true, to_apply=%add | all-reduce | flops 128 | bytes 1024
  210.9 0.0 copy-done.6
  210.9 0.1 select_reduce_fusion
  211.0 0.6 fusion.23
  212.3 0.0 copy-done.3
  212.3 0.6 convolution_multiply_fusion.1
  212.9 0.0 copy-done.4
  212.9 2.0 convolution_multiply_fusion
  214.9 187.2 %reduce-scatter.8.cloned.1.call-done = f32[1,16,128]{2,1,0:T(8,128)} async-done(((f32[32,16,128]{2,1,0:T(8,128)}), f32[1,16,128]{2,1,0:T(8,128)}) %reduce-scatter.8.cloned.1.call-update) | async-done | bytes 8208 | tf_op jit(solution)/shard_map/reduce_scatter | solution.py:94
  402.1 1.3 broadcast_multiply_fusion.1
  403.4 224.2 %reduce-scatter.6.cloned.1.call-done = f32[1,16,512]{2,1,0:T(8,128)} async-done(((f32[32,16,512]{2,1,0:T(8,128)}), f32[1,16,512]{2,1,0:T(8,128)}) %reduce-scatter.6.cloned.1.call-update) | async-done | bytes 32784 | tf_op jit(solution)/shard_map/reduce_scatter | solution.py:93
  627.6 1.4 broadcast_multiply_fusion
  629.0 46.8 %all-gather.2.cloned.1.call-done = bf16[512,2048]{1,0:T(8,128)(2,1)} async-done(((bf16[512,128]{1,0:T(8,128)(2,1)}), bf16[512,2048]{1,0:T(8,128)(2,1)}) %all-gather.2.cloned.1.call-update) | async-done | bytes 2097168 | tf_op jit(solution)/shard_map/all_gather | solution.py:65
  675.8 4.1 convolution_add_fusion
  679.9 64.2 %reduce-scatter.4.cloned.1.call-done = f32[512,128]{1,0:T(8,128)} async-done(((f32[512,2048]{1,0:T(8,128)}), f32[512,128]{1,0:T(8,128)}) %reduce-scatter.4.cloned.1.call-update) | async-done | bytes 262160 | tf_op jit(solution)/shard_map/reduce_scatter | solution.py:61
  744.1 1.7 bitcast_add_fusion
  (1 shorter events, 0.0 us)
Async XLA Ops:
  7.2 181.0 %copy-start = (bf16[512,2048]{1,0:T(8,128)(2,1)S(1)}, bf16[512,2048]{1,0:T(8,128)(2,1)}, u32[]{:S(2)}) copy-start(bf16[512,2048]{1,0:T(8,128)(2,1)} %param.8) | copy-start | bytes 6291460
  7.2 176.9 %copy-start.1 = (bf16[512,512]{1,0:T(8,128)(2,1)S(1)}, bf16[512,512]{1,0:T(8,128)(2,1)}, u32[]{:S(2)}) copy-start(bf16[512,512]{1,0:T(8,128)(2,1)} %param.7) | copy-start | bytes 1572868
  7.2 56.8 %copy-start.2 = (bf16[512,128]{1,0:T(8,128)(2,1)S(1)}, bf16[512,128]{1,0:T(8,128)(2,1)}, u32[]{:S(2)}) copy-start(bf16[512,128]{1,0:T(8,128)(2,1)} %param.9) | copy-start | bytes 393220
  8.7 55.0 %all-to-all-start = ((bf16[32,1,16,128]{3,2,1,0:T(8,128)(2,1)}), bf16[32,1,16,128]{3,2,1,0:T(8,128)(2,1)S(1)}, u32[]{:S(2)}, u32[]{:S(2)}) async-start(bf16[32,1,16,128]{3,2,1,0:T(8,128)(2,1)} %stack.2), calls=%async_computation.1 | async-start | bytes 262144 | tf_op jit(solution)/shard_map/all_to_all | solution.py:11
  21.6 160.1 %all-reduce.4.cloned.1.call-start = ((), (), s32[]{:S(2)}) async-start(), calls=%async_computation.8 | async-start | bytes 131072 | tf_op jit(solution)/shard_map/psum | solution.py:59
  64.9 337.2 %reduce-scatter.8.cloned.1.call-start = ((), (), s32[]{:S(2)}) async-start(), calls=%async_computation.7 | async-start | bytes 270336 | tf_op jit(solution)/shard_map/reduce_scatter | solution.py:94
  184.0 443.6 %reduce-scatter.6.cloned.1.call-start = ((), (), s32[]{:S(2)}) async-start(), calls=%async_computation.6 | async-start | bytes 1081344 | tf_op jit(solution)/shard_map/reduce_scatter | solution.py:93
  187.5 488.3 %all-gather.2.cloned.1.call-start = ((), (), s32[]{:S(2)}) async-start(), calls=%async_computation.5 | async-start | bytes 2228224 | tf_op jit(solution)/shard_map/all_gather | solution.py:65
  188.1 556.0 %reduce-scatter.4.cloned.1.call-start = ((), (), s32[]{:S(2)}) async-start(), calls=%async_computation.4 | async-start | bytes 4456448 | tf_op jit(solution)/shard_map/reduce_scatter | solution.py:61
  191.3 2.0 copy-start.5
  191.3 19.6 %copy-start.6 = (s32[32]{0:T(128)S(1)}, s32[32]{0:T(128)}, u32[]{:S(2)}) copy-start(s32[32]{0:T(128)} %param.13) | copy-start | bytes 388
  191.3 21.0 %copy-start.3 = (f32[4,128,16]{1,2,0:T(8,128)S(1)}, f32[4,128,16]{1,2,0:T(8,128)}, u32[]{:S(2)}) copy-start(f32[4,128,16]{1,2,0:T(8,128)} %get-tuple-element.8) | copy-start | bytes 98308
  191.3 21.6 %copy-start.4 = (f32[4,128,16]{1,2,0:T(8,128)S(1)}, f32[4,128,16]{1,2,0:T(8,128)}, u32[]{:S(2)}) copy-start(f32[4,128,16]{1,2,0:T(8,128)} %get-tuple-element.9) | copy-start | bytes 98308
Sparse Core Ops, SparseCore 0:
  65.1 116.6 all-reduce.3
  186.7 215.3 reduce-scatter.7
  406.5 221.0 reduce-scatter.5
  629.5 46.2 all-gather.1
  678.4 65.6 reduce-scatter.3
